TPU v7x, 32 devices: a whole 2x2x4 slice. The times are simulated.
32 devices in a mesh: dp: 4 (over z), fsdp: 8 (over y, x, core).
Axes of the slice: x: 2, y: 2, z: 4, core: 2. Of those that a mesh axis runs over, the one named last changes fastest.
Arguments:
- block_input: bfloat16 [2, 32, 576, 768], P(None, ('dp', 'fsdp')), may hold values from -6 to 6
- valid_counts: int32 [2, 32], P(None, ('dp', 'fsdp')), may hold values from 288 to 576
- output_cotangent: bfloat16 [2, 32, 576, 768], P(None, ('dp', 'fsdp')), may hold values from -6 to 6
- triple_weight: float32 [768, 2304], P(('dp', 'fsdp')), may hold values from -0.21875 to 0.21875
- merge_weight: float32 [768, 768], P(('dp', 'fsdp')), may hold values from -0.875 to 0.875
- expand_weight: float32 [768, 3072], P(('dp', 'fsdp')), may hold values from -0.21875 to 0.21875
- reduce_weight: float32 [3072, 768], P(('dp', 'fsdp')), may hold values from -0.109375 to 0.109375
- first_gain: float32 [768], P(('dp', 'fsdp')), may hold values from 0.25 to 1.75
- first_shift: float32 [768], P(('dp', 'fsdp')), may hold values from -3 to 3
- query_bias: float32 [768], P(('dp', 'fsdp')), may hold values from -3 to 3
- value_bias: float32 [768], P(('dp', 'fsdp')), may hold values from -3 to 3
- merge_bias: float32 [768], P(('dp', 'fsdp')), may hold values from -3 to 3
- second_gain: float32 [768], P(('dp', 'fsdp')), may hold values from 0.25 to 1.75
- second_shift: float32 [768], P(('dp', 'fsdp')), may hold values from -3 to 3
- expand_bias: float32 [3072], P(('dp', 'fsdp')), may hold values from -3 to 3
- reduce_bias: float32 [768], P(('dp', 'fsdp')), may hold values from -3 to 3
- position_table: float32 [529, 24], replicated, may hold values from -4 to 4
Outputs:
- block_output: bfloat16 [2, 32, 576, 768], P(None, ('dp', 'fsdp'))
- input_grad: bfloat16 [2, 32, 576, 768], P(None, ('dp', 'fsdp'))
- triple_grad: float32 [768, 2304], P(('dp', 'fsdp'))
- merge_grad: float32 [768, 768], P(('dp', 'fsdp'))
- expand_grad: float32 [768, 3072], P(('dp', 'fsdp'))
- reduce_grad: float32 [3072, 768], P(('dp', 'fsdp'))
- first_gain_grad: float32 [768], P(('dp', 'fsdp'))
- first_shift_grad: float32 [768], P(('dp', 'fsdp'))
- query_bias_grad: float32 [768], P(('dp', 'fsdp'))
- value_bias_grad: float32 [768], P(('dp', 'fsdp'))
- merge_bias_grad: float32 [768], P(('dp', 'fsdp'))
- second_gain_grad: float32 [768], P(('dp', 'fsdp'))
- second_shift_grad: float32 [768], P(('dp', 'fsdp'))
- expand_bias_grad: float32 [3072], P(('dp', 'fsdp'))
- reduce_bias_grad: float32 [768], P(('dp', 'fsdp'))
- position_table_grad: float32 [529, 24], replicated
Inputs may be any that keep to these rules, and one draw needn't show every extreme that they name: `valid_counts`: tokens at raster positions from the count on are padding: they are no keys, and their attention output is zero.
All inputs are finite; a program needn't handle non-finite values.
Results may differ from a plain program's by a relative error of at most 0.012.
The roundings to bfloat16 on the way count: a program that leaves them out, or rounds other values in their place, can miss the bound.
Values may be sent and summed in bfloat16 or wider, within the bound.
A program may use at most 192 MiB of HBM per device.

v0:
```python
import math

import jax
import jax.numpy as jnp
from jax import lax
from jax.sharding import PartitionSpec as P

D = 768
FF = 3072
HEADS = 24
HEAD_DIM = 32
WIN = 12
SIDE = 24
SHIFT = 6


PRECISE = lax.Precision.HIGHEST
MASKED_SCORE = -1000000000.0
NORM_EPSILON = 1e-05
HALF_ROOT = 1.0 / math.sqrt(2.0)
GAUSS_FACTOR = 1.0 / math.sqrt(2.0 * math.pi)


def partition(token_grid):
    across = SIDE // WIN
    channels = token_grid.shape[-1]
    shaped = token_grid.reshape(across, WIN, across, WIN, channels).transpose(0, 2, 1, 3, 4)
    return shaped.reshape(across * across, WIN * WIN, channels)


def window_order(tokens):
    token_grid = tokens.reshape(SIDE, SIDE, tokens.shape[-1])
    return partition(jnp.roll(token_grid, (-SHIFT, -SHIFT), (0, 1)))


def grid_order(windows):
    across = SIDE // WIN
    channels = windows.shape[-1]
    token_grid = windows.reshape(across, across, WIN, WIN, channels).transpose(0, 2, 1, 3, 4)
    token_grid = token_grid.reshape(SIDE, SIDE, channels)
    return jnp.roll(token_grid, (SHIFT, SHIFT), (0, 1)).reshape(SIDE * SIDE, channels)


def offset_onehot():
    query_pos = jnp.arange(WIN)[:, None, None]
    key_pos = jnp.arange(WIN)[None, :, None]
    target_pos = jnp.arange(2 * WIN - 1)[None, None, :]
    return (query_pos - key_pos + WIN - 1 == target_pos).astype(jnp.float32)


def relative_bias(position_table):
    onehot = offset_onehot()
    extent = 2 * WIN - 1
    table_cube = position_table.reshape(extent, extent, HEADS)
    partial_sum = jnp.einsum("cds,rsh->cdrh", onehot, table_cube, precision=PRECISE)
    bias_full = jnp.einsum("abr,cdrh->hacbd", onehot, partial_sum, precision=PRECISE)
    return bias_full.reshape(HEADS, WIN * WIN, WIN * WIN)


def table_gradient(bias_grad):
    onehot = offset_onehot()
    extent = 2 * WIN - 1
    bias_cube = bias_grad.reshape(HEADS, WIN, WIN, WIN, WIN)
    partial_sum = jnp.einsum("abr,hacbd->cdrh", onehot, bias_cube, precision=PRECISE)
    table_cube = jnp.einsum("cds,cdrh->rsh", onehot, partial_sum, precision=PRECISE)
    return table_cube.reshape(extent * extent, HEADS)


def region_labels():
    coords = jnp.arange(SIDE)
    region = (coords >= SIDE - WIN).astype(jnp.int32) + (coords >= SIDE - SHIFT).astype(jnp.int32)
    labels = region[:, None] * 3 + region[None, :]
    return partition(labels[:, :, None])[:, :, 0]


def token_masks(labels, valid_count):
    valid_mask = (jnp.arange(SIDE * SIDE) < valid_count).astype(jnp.float32)
    valid_win = window_order(valid_mask[:, None])[:, :, 0]
    allowed = (labels[:, :, None] == labels[:, None, :]) & (valid_win[:, None, :] > 0.5)
    return (valid_win, allowed)


def layer_norm(values, gain_row, shift_row):
    center = values - jnp.mean(values, axis=-1, keepdims=True)
    spread = jnp.mean(center * center, axis=-1, keepdims=True)
    return center * lax.rsqrt(spread + NORM_EPSILON) * gain_row + shift_row


def norm_back(values, gain_row, grad_out):
    center = values - jnp.mean(values, axis=-1, keepdims=True)
    spread = jnp.mean(center * center, axis=-1, keepdims=True)
    inverse = lax.rsqrt(spread + NORM_EPSILON)
    normal = center * inverse
    gain_grad = jnp.sum(grad_out * normal, axis=0)
    shift_grad = jnp.sum(grad_out, axis=0)
    scaled = grad_out * gain_row
    back = inverse * (
        scaled
        - jnp.mean(scaled, axis=-1, keepdims=True)
        - normal * jnp.mean(scaled * normal, axis=-1, keepdims=True)
    )
    return (back, gain_grad, shift_grad)


def gelu_slope(hidden):
    return (
        0.5 * (1.0 + lax.erf(hidden * HALF_ROOT))
        + hidden * jnp.exp(-0.5 * hidden * hidden) * GAUSS_FACTOR
    )


def contract_rows(left_rows, right_rows):
    return lax.dot_general(
        left_rows, right_rows, (((0,), (0,)), ((), ())), preferred_element_type=jnp.float32
    )


def times_transposed(left_rows, weight):
    return lax.dot_general(
        left_rows, weight, (((1,), (1,)), ((), ())), preferred_element_type=jnp.float32
    )


def split_heads(windows):
    across = windows.shape[0]

    def head_slice(offset):
        return windows[:, :, offset * D : (offset + 1) * D].reshape(
            across, WIN * WIN, HEADS, HEAD_DIM
        )

    return (head_slice(0), head_slice(1), head_slice(2))


def masked_scores(queries, keys_win, pos_bias, allowed):
    raw_scores = jnp.einsum(
        "wqhd,wkhd->whqk", queries, keys_win, preferred_element_type=jnp.float32
    )
    scores = raw_scores * float(HEAD_DIM) ** (-0.5) + pos_bias[None]
    return jnp.where(allowed[:, None], scores, MASKED_SCORE)


def forward_image(weights, pos_bias, labels, image_rows, valid_count):
    triple_w, merge_w, expand_w, reduce_w, small_w, expand_b = weights
    gains = small_w.astype(jnp.float32)
    image_wide = image_rows.astype(jnp.float32)
    normed = layer_norm(image_wide, gains[0], gains[1]).astype(jnp.bfloat16)
    triple_bias = jnp.concatenate([gains[2], jnp.zeros_like(gains[2]), gains[3]])
    triple = (jnp.dot(normed, triple_w, preferred_element_type=jnp.float32) + triple_bias).astype(
        jnp.bfloat16
    )
    windows = window_order(triple)
    valid_win, allowed = token_masks(labels, valid_count)
    queries, keys_win, values_win = split_heads(windows)
    scores = masked_scores(queries, keys_win, pos_bias, allowed)
    row_peak = jnp.max(scores, axis=-1, keepdims=True)
    exp_scores = jnp.exp(scores - row_peak)
    row_total = jnp.sum(exp_scores, axis=-1, keepdims=True)
    attention = (exp_scores / row_total).astype(jnp.bfloat16)
    log_total = row_peak + jnp.log(row_total)
    attended = jnp.einsum(
        "whqk,wkhd->wqhd", attention, values_win, preferred_element_type=jnp.float32
    )
    attended = attended.reshape(windows.shape[0], WIN * WIN, D) * valid_win[:, :, None]
    attended = grid_order(attended).astype(jnp.bfloat16)
    mixed_rows = (
        image_wide + jnp.dot(attended, merge_w, preferred_element_type=jnp.float32) + gains[4]
    )
    normed_two = layer_norm(mixed_rows, gains[5], gains[6]).astype(jnp.bfloat16)
    hidden = jnp.dot(normed_two, expand_w, preferred_element_type=jnp.float32) + expand_b.astype(
        jnp.float32
    )
    active = jax.nn.gelu(hidden, approximate=False).astype(jnp.bfloat16)
    output = (
        mixed_rows + jnp.dot(active, reduce_w, preferred_element_type=jnp.float32) + gains[7]
    ).astype(jnp.bfloat16)
    return (output, (normed, windows, log_total, attended, mixed_rows, normed_two, hidden, active))


def backward_image(weights, pos_bias, labels, image_rows, valid_count, cotangent, image_state):
    triple_w, merge_w, expand_w, reduce_w, small_w, expand_b = weights
    normed, windows, log_total, attended, mixed_rows, normed_two, hidden, active = image_state
    gains = small_w.astype(jnp.float32)
    out_grad = cotangent.astype(jnp.float32)
    reduce_w_grad = contract_rows(active, cotangent)
    reduce_bias_grad = jnp.sum(out_grad, axis=0)
    hidden_grad = times_transposed(cotangent, reduce_w) * gelu_slope(hidden)
    hidden_low = hidden_grad.astype(jnp.bfloat16)
    expand_w_grad = contract_rows(normed_two, hidden_low)
    expand_bias_grad = jnp.sum(hidden_grad, axis=0)
    normed_two_grad = times_transposed(hidden_low, expand_w)
    mixed_back, second_gain_grad, second_shift_grad = norm_back(
        mixed_rows, gains[5], normed_two_grad
    )
    mixed_grad = out_grad + mixed_back
    mixed_low = mixed_grad.astype(jnp.bfloat16)
    merge_w_grad = contract_rows(attended, mixed_low)
    merge_bias_grad = jnp.sum(mixed_grad, axis=0)
    attended_grad = times_transposed(mixed_low, merge_w).astype(jnp.bfloat16)
    valid_win, allowed = token_masks(labels, valid_count)
    across = windows.shape[0]
    attended_heads = (
        window_order(attended_grad) * valid_win[:, :, None].astype(jnp.bfloat16)
    ).reshape(across, WIN * WIN, HEADS, HEAD_DIM)
    queries, keys_win, values_win = split_heads(windows)
    scores = masked_scores(queries, keys_win, pos_bias, allowed)
    attention = jnp.exp(scores - log_total)
    attention_low = attention.astype(jnp.bfloat16)
    values_grad = jnp.einsum(
        "whqk,wqhd->wkhd", attention_low, attended_heads, preferred_element_type=jnp.float32
    )
    attention_grad = jnp.einsum(
        "wqhd,wkhd->whqk", attended_heads, values_win, preferred_element_type=jnp.float32
    )
    row_inner = jnp.sum(attention * attention_grad, axis=-1, keepdims=True)
    scores_grad = attention * (attention_grad - row_inner)
    bias_grad = jnp.sum(scores_grad, axis=0)
    raw_low = (scores_grad * float(HEAD_DIM) ** (-0.5)).astype(jnp.bfloat16)
    queries_grad = jnp.einsum(
        "whqk,wkhd->wqhd", raw_low, keys_win, preferred_element_type=jnp.float32
    )
    keys_grad = jnp.einsum("whqk,wqhd->wkhd", raw_low, queries, preferred_element_type=jnp.float32)
    triple_grad_win = jnp.concatenate(
        [
            queries_grad.reshape(across, WIN * WIN, D),
            keys_grad.reshape(across, WIN * WIN, D),
            values_grad.reshape(across, WIN * WIN, D),
        ],
        axis=-1,
    )
    triple_low = grid_order(triple_grad_win).astype(jnp.bfloat16)
    triple_w_grad = contract_rows(normed, triple_low)
    column_sums = jnp.sum(triple_low, axis=0, dtype=jnp.float32)
    normed_grad = times_transposed(triple_low, triple_w)
    image_back, first_gain_grad, first_shift_grad = norm_back(
        image_rows.astype(jnp.float32), gains[0], normed_grad
    )
    input_grad = (mixed_grad + image_back).astype(jnp.bfloat16)
    small_grad = jnp.stack(
        [
            first_gain_grad,
            first_shift_grad,
            column_sums[:D],
            column_sums[2 * D :],
            merge_bias_grad,
            second_gain_grad,
            second_shift_grad,
            reduce_bias_grad,
        ]
    )
    return (
        input_grad,
        (
            triple_w_grad,
            merge_w_grad,
            expand_w_grad,
            reduce_w_grad,
            small_grad,
            expand_bias_grad,
            bias_grad,
        ),
    )


def forward_micro(weights, pos_bias, labels, images, counts_row):

    def forward_one_image(image_entry):
        return forward_image(weights, pos_bias, labels, image_entry[0], image_entry[1])

    return lax.map(forward_one_image, (images, counts_row))


def backward_micro(weights, pos_bias, labels, images, counts_row, cotangents, kept_state, totals):

    def backward_one_image(running, image_entry):
        image_rows, valid_count, cotangent, image_state = image_entry
        input_grad, parts = backward_image(
            weights, pos_bias, labels, image_rows, valid_count, cotangent, image_state
        )
        return (
            tuple((left_part + right_part for left_part, right_part in zip(running, parts))),
            input_grad,
        )

    return lax.scan(backward_one_image, totals, (images, counts_row, cotangents, kept_state))


def shards(
    block_input,
    valid_counts,
    output_cotangent,
    triple_weight,
    merge_weight,
    expand_weight,
    reduce_weight,
    first_gain,
    first_shift,
    query_bias,
    value_bias,
    merge_bias,
    second_gain,
    second_shift,
    expand_bias,
    reduce_bias,
    position_table,
):
    micro_count = block_input.shape[0]
    small_master = jnp.stack(
        [
            first_gain,
            first_shift,
            query_bias,
            value_bias,
            merge_bias,
            second_gain,
            second_shift,
            reduce_bias,
        ]
    )
    triple_send = triple_weight.astype(jnp.bfloat16)
    merge_send = merge_weight.astype(jnp.bfloat16)
    expand_send = expand_weight.astype(jnp.bfloat16)
    reduce_send = reduce_weight.astype(jnp.bfloat16)
    small_send = small_master.astype(jnp.bfloat16)
    expand_bias_send = expand_bias.astype(jnp.bfloat16)
    pos_bias = relative_bias(position_table)
    labels = region_labels()
    outputs = []
    kept_list = []
    for micro_index in range(micro_count):
        weights = (
            lax.all_gather(triple_send, ("dp", "fsdp"), axis=0, tiled=True),
            lax.all_gather(merge_send, ("dp", "fsdp"), axis=0, tiled=True),
            lax.all_gather(expand_send, ("dp", "fsdp"), axis=0, tiled=True),
            lax.all_gather(reduce_send, ("dp", "fsdp"), axis=0, tiled=True),
            lax.all_gather(small_send, ("dp", "fsdp"), axis=1, tiled=True),
            lax.all_gather(expand_bias_send, ("dp", "fsdp"), axis=0, tiled=True),
        )
        output, kept_state = forward_micro(
            weights, pos_bias, labels, block_input[micro_index], valid_counts[micro_index]
        )
        outputs.append(output)
        kept_list.append(kept_state)
    zeros_all = (
        jnp.zeros((D, 3 * D), jnp.float32),
        jnp.zeros((D, D), jnp.float32),
        jnp.zeros((D, FF), jnp.float32),
        jnp.zeros((FF, D), jnp.float32),
        jnp.zeros((8, D), jnp.float32),
        jnp.zeros((FF,), jnp.float32),
        jnp.zeros((HEADS, WIN * WIN, WIN * WIN), jnp.float32),
    )
    totals = zeros_all
    input_grads = []
    for micro_index in range(micro_count):
        weights = (
            lax.all_gather(triple_send, ("dp", "fsdp"), axis=0, tiled=True),
            lax.all_gather(merge_send, ("dp", "fsdp"), axis=0, tiled=True),
            lax.all_gather(expand_send, ("dp", "fsdp"), axis=0, tiled=True),
            lax.all_gather(reduce_send, ("dp", "fsdp"), axis=0, tiled=True),
            lax.all_gather(small_send, ("dp", "fsdp"), axis=1, tiled=True),
            lax.all_gather(expand_bias_send, ("dp", "fsdp"), axis=0, tiled=True),
        )
        totals, input_grad = backward_micro(
            weights,
            pos_bias,
            labels,
            block_input[micro_index],
            valid_counts[micro_index],
            output_cotangent[micro_index],
            kept_list[micro_index],
            totals,
        )
        input_grads.append(input_grad)
    shares = (
        lax.psum_scatter(totals[0], ("dp", "fsdp"), scatter_dimension=0, tiled=True),
        lax.psum_scatter(totals[1], ("dp", "fsdp"), scatter_dimension=0, tiled=True),
        lax.psum_scatter(totals[2], ("dp", "fsdp"), scatter_dimension=0, tiled=True),
        lax.psum_scatter(totals[3], ("dp", "fsdp"), scatter_dimension=0, tiled=True),
        lax.psum_scatter(totals[4], ("dp", "fsdp"), scatter_dimension=1, tiled=True),
        lax.psum_scatter(totals[5], ("dp", "fsdp"), scatter_dimension=0, tiled=True),
    )
    table_sum = lax.psum(table_gradient(totals[6]), ("dp", "fsdp"))
    small_share = shares[4]
    return (
        jnp.stack(outputs),
        jnp.stack(input_grads),
        shares[0],
        shares[1],
        shares[2],
        shares[3],
        small_share[0],
        small_share[1],
        small_share[2],
        small_share[3],
        small_share[4],
        small_share[5],
        small_share[6],
        shares[5],
        small_share[7],
        table_sum,
    )


def solution(mesh):
    placed = (
        P(None, ("dp", "fsdp"), None, None),
        P(None, ("dp", "fsdp")),
        P(None, ("dp", "fsdp"), None, None),
        P(("dp", "fsdp"), None),
        P(("dp", "fsdp"), None),
        P(("dp", "fsdp"), None),
        P(("dp", "fsdp"), None),
        P(("dp", "fsdp")),
        P(("dp", "fsdp")),
        P(("dp", "fsdp")),
        P(("dp", "fsdp")),
        P(("dp", "fsdp")),
        P(("dp", "fsdp")),
        P(("dp", "fsdp")),
        P(("dp", "fsdp")),
        P(("dp", "fsdp")),
        P(),
    )
    return jax.shard_map(
        shards,
        mesh=mesh,
        in_specs=placed,
        out_specs=(
            P(None, ("dp", "fsdp"), None, None),
            P(None, ("dp", "fsdp"), None, None),
            P(("dp", "fsdp"), None),
            P(("dp", "fsdp"), None),
            P(("dp", "fsdp"), None),
            P(("dp", "fsdp"), None),
            P(("dp", "fsdp")),
            P(("dp", "fsdp")),
            P(("dp", "fsdp")),
            P(("dp", "fsdp")),
            P(("dp", "fsdp")),
            P(("dp", "fsdp")),
            P(("dp", "fsdp")),
            P(("dp", "fsdp")),
            P(("dp", "fsdp")),
            P(),
        ),
        check_vma=False,
    )
```

profile of v0, /device:TPU:0, one launch (start us, length us, event | category | flops | bytes accessed | tf_op | source)
XLA Modules:
  0.0 1340.5 jit_solution(15124571099202562572)
XLA Ops:
  18.2 42.1 %all-reduce = bf16[3072]{0:T(1024)(128)(2,1)S(1)} all-reduce(bf16[3072]{0:T(1024)(128)(2,1)S(1)} %dynamic-update-slice), channel_id=1, replica_groups=mesh['dp'=4,'fsdp'=8] {'dp','fsdp'}, use_global_device_ids=true, to_apply=%add | all-reduce | flops 3072 | bytes 12288
  67.1 40.5 %all-gather = bf16[32,24,8]{1,2,0:T(8,128)(2,1)S(1)} all-gather(bf16[1,24,8]{1,2,0:T(8,128)(2,1)S(1)} %bitcast.405), channel_id=1, replica_groups=mesh['dp'=4,'fsdp'=8] {'dp','fsdp'}, dimensions={0}, use_global_device_ids=true | all-gather | bytes 12672 | tf_op jit(solution)/shard_map/all_gather | solution.py:336
  111.9 9.0 convolution_bitcast_fusion
  120.9 16.4 %copy.199 = f32[24,12,12,12,12]{0,4,3,2,1:T(8,128)} copy(f32[24,12,12,12,12]{0,3,1,4,2:T(8,128)} %convolution_bitcast_fusion) | data formatting | bytes 3981312 | tf_op jit(solution)/shard_map/abr,cdrh->hacbd/transpose | solution.py:56
  137.4 13.0 add.440
  150.4 12.2 copy.200
  211.6 10.4 fusion.213
  222.0 9.0 fusion.9
  231.6 9.4 fusion.78
  299.8 10.3 fusion.214
  346.8 8.9 fusion.203
  370.4 36.1 %fusion.14 = (bf16[576,3072]{1,0:T(8,128)(2,1)}, bf16[576,3072]{1,0:T(8,128)(2,1)}, f32[576,3072]{1,0:T(8,128)}) fusion(f32[3072]{0:T(1024)S(1)} %copy-done.95, f32[576,3072]{1,0:T(8,128)S(1)} %copy-done.123, bf16[768,3072]{1,0:T(8,128)(2,1)S(1)} %copy-done.118, f32[576,768]{1,0:T(8,128)S(1)} %get-tuple-element.382, f32[768]{0:T(1024)S(1)} %get-tuple-element.269, ...), kind=kOutput, calls=%fused_computation.29 | convolution fusion | flops 2953691136 | bytes 27744768 | tf_op jit(solution)/shard_map/while/body/eval_jaxpr/dot_general | solution.py:170
  449.7 20.1 %fusion.219 = (f32[24,144,144]{1,2,0:T(8,128)}, f32[4,24,144,144]{2,3,1,0:T(8,128)}) fusion(f32[4,24,144,144]{2,3,1,0:T(8,128)} %get-tuple-element.380, f32[4,24,144]{2,1,0:T(8,128)S(1)} %copy-done.46, bf16[4,144,24,32]{1,3,2,0:T(8,128)(2,1)S(1)} %copy.217, bf16[4,144,24,32]{1,3,2,0:T(8,128)(2,1)S(1)} %bitcast.365), kind=kOutput, calls=%fused_computation.358 | convolution fusion | flops 266264208 | bytes 19740672 | tf_op jit(solution)/shard_map/while/body/eval_jaxpr/sub | solution.py:216
  469.8 9.1 fusion.89
  534.7 19.7 %fusion.220 = (f32[24,144,144]{1,2,0:T(8,128)}, f32[4,24,144,144]{2,3,1,0:T(8,128)}) fusion(f32[4,24,144,144]{2,3,1,0:T(8,128)} %get-tuple-element.378, f32[4,24,144]{2,1,0:T(8,128)S(1)} %copy-done.45, bf16[4,144,24,32]{1,3,2,0:T(8,128)(2,1)S(1)} %copy.229, bf16[4,144,24,32]{1,3,2,0:T(8,128)(2,1)S(1)} %bitcast.363), kind=kOutput, calls=%fused_computation.359 | convolution fusion | flops 266264208 | bytes 19740672 | tf_op jit(solution)/shard_map/while/body/eval_jaxpr/sub | solution.py:216
  554.4 9.1 fusion.87
  618.8 18.5 %reshape.618 = f32[24,12,12,12,12]{2,1,4,3,0:T(8,128)} reshape(f32[24,144,144]{1,2,0:T(8,128)} %add.487) | data formatting | bytes 3981312 | tf_op jit(solution)/shard_map/while/body/eval_jaxpr/add | solution.py:281
  637.4 32.6 %copy.239 = f32[24,12,12,12,12]{0,3,1,4,2:T(8,128)} copy(f32[24,12,12,12,12]{2,1,4,3,0:T(8,128)} %reshape.618) | data formatting | bytes 3981312 | tf_op jit(solution)/shard_map/while/body/eval_jaxpr/add | solution.py:281
  669.9 14.8 %convolution_bitcast_fusion.2 = f32[12,12,23,24]{2,3,1,0:T(8,128)S(1)} fusion(f32[24,12,12,12,12]{0,3,1,4,2:T(8,128)} %copy.239, s32[12,12]{1,0:T(8,128)S(1)} %copy-done.67), kind=kOutput, calls=%fused_computation.206 | convolution fusion | flops 137358576 | bytes 2309184 | tf_op jit(solution)/shard_map/abr,hacbd->cdrh/dot_general | solution.py:64
  761.5 56.3 %all-reduce.6.cloned.1.call-done = (f32[8,768]{1,0:T(8,128)}, f32[3072]{0:T(1024)}, f32[529,24]{0,1:T(8,128)}) async-done(((f32[8,768]{1,0:T(8,128)}, f32[3072]{0:T(1024)}, f32[529,24]{0,1:T(8,128)}), (f32[8,768]{1,0:T(8,128)}, f32[3072]{0:T(1024)}, f32[529,24]{0,1:T(8,128)})) %all-reduce.6.cloned.1.call-update) | async-done | bytes 87664
  820.4 103.1 %reduce-scatter.8.cloned.1.call-done = f32[24,768]{1,0:T(8,128)} async-done(((f32[768,768]{1,0:T(8,128)}), f32[24,768]{1,0:T(8,128)}) %reduce-scatter.8.cloned.1.call-update) | async-done | bytes 73744 | tf_op jit(solution)/shard_map/reduce_scatter | solution.py:377
  923.5 125.2 %reduce-scatter.6.cloned.1.call-done = f32[24,2304]{1,0:T(8,128)} async-done(((f32[768,2304]{1,0:T(8,128)}), f32[24,2304]{1,0:T(8,128)}) %reduce-scatter.6.cloned.1.call-update) | async-done | bytes 221200 | tf_op jit(solution)/shard_map/reduce_scatter | solution.py:376
  1048.7 141.4 %reduce-scatter.10.cloned.1.call-done = f32[24,3072]{1,0:T(8,128)} async-done(((f32[768,3072]{1,0:T(8,128)}), f32[24,3072]{1,0:T(8,128)}) %reduce-scatter.10.cloned.1.call-update) | async-done | bytes 294928 | tf_op jit(solution)/shard_map/reduce_scatter | solution.py:378
  1190.1 142.2 %reduce-scatter.12.cloned.1.call-done = f32[96,768]{1,0:T(8,128)} async-done(((f32[3072,768]{1,0:T(8,128)}), f32[96,768]{1,0:T(8,128)}) %reduce-scatter.12.cloned.1.call-update) | async-done | bytes 294928 | tf_op jit(solution)/shard_map/reduce_scatter | solution.py:379
  (498 shorter events, 415.1 us)
Async XLA Ops:
  7.2 158.5 %all-gather.6.cloned.1.call-start = ((), (), s32[]{:S(2)}) async-start(), calls=%async_computation.4 | async-start | bytes 3649536 | tf_op jit(solution)/shard_map/all_gather | solution.py:332
  9.0 331.2 %all-gather.8.cloned.1.call-start = ((), (), s32[]{:S(2)}) async-start(), calls=%async_computation.5 | async-start | bytes 1216512 | tf_op jit(solution)/shard_map/all_gather | solution.py:333
  10.6 336.3 %all-gather.10.cloned.1.call-start = ((), (), s32[]{:S(2)}) async-start(), calls=%async_computation.6 | async-start | bytes 4866048 | tf_op jit(solution)/shard_map/all_gather | solution.py:334
  12.2 54.7 %copy-start.111 = (f32[24]{0:T(128)S(1)}, f32[24]{0:T(128)}, u32[]{:S(2)}) copy-start(f32[24]{0:T(128)} %param.27) | copy-start | bytes 292
  12.3 54.8 %copy-start.112 = (f32[24]{0:T(128)S(1)}, f32[24]{0:T(128)}, u32[]{:S(2)}) copy-start(f32[24]{0:T(128)} %param.26) | copy-start | bytes 292
  12.3 54.8 %copy-start.113 = (f32[24]{0:T(128)S(1)}, f32[24]{0:T(128)}, u32[]{:S(2)}) copy-start(f32[24]{0:T(128)} %param.29) | copy-start | bytes 292
  12.3 54.8 %copy-start.114 = (f32[24]{0:T(128)S(1)}, f32[24]{0:T(128)}, u32[]{:S(2)}) copy-start(f32[24]{0:T(128)} %param.28) | copy-start | bytes 292
  12.3 54.8 %copy-start.115 = (f32[24]{0:T(128)S(1)}, f32[24]{0:T(128)}, u32[]{:S(2)}) copy-start(f32[24]{0:T(128)} %param.32) | copy-start | bytes 292
  12.3 54.8 %copy-start.116 = (f32[24]{0:T(128)S(1)}, f32[24]{0:T(128)}, u32[]{:S(2)}) copy-start(f32[24]{0:T(128)} %param.30) | copy-start | bytes 292
  12.3 343.4 %all-gather.12.cloned.1.call-start = ((), (), s32[]{:S(2)}) async-start(), calls=%async_computation.7 | async-start | bytes 4866048 | tf_op jit(solution)/shard_map/all_gather | solution.py:335
  14.0 803.8 %all-reduce.6.cloned.1.call-start = ((), (), s32[]{:S(2)}) async-start(), calls=%async_computation.12 | async-start | bytes 196608
  14.1 97.8 %copy-start.66 = (s32[12,12]{1,0:T(8,128)}, s32[12,12]{1,0:T(8,128)S(1)}, u32[]{:S(2)}) copy-start(s32[12,12]{1,0:T(8,128)S(1)} %subtract_add_fusion) | copy-start | bytes 1732
  16.8 93.7 %copy-start.73 = (f32[529,24]{0,1:T(8,128)S(1)}, f32[529,24]{0,1:T(8,128)}, u32[]{:S(2)}) copy-start(f32[529,24]{0,1:T(8,128)} %param.33) | copy-start | bytes 152356
  61.3 104.4 %copy-start.74 = (f32[576]{0:T(1024)}, f32[576]{0:T(1024)S(1)}, u32[]{:S(2)}) copy-start(f32[576]{0:T(1024)S(1)} %get-tuple-element.404) | copy-start | bytes 6916
  61.3 109.5 %copy-start.77 = (f32[576]{0:T(1024)}, f32[576]{0:T(1024)S(1)}, u32[]{:S(2)}) copy-start(f32[576]{0:T(1024)S(1)} %get-tuple-element.405) | copy-start | bytes 6916
  108.6 261.7 %copy-start.56 = (f32[768]{0:T(1024)}, f32[768]{0:T(1024)S(1)}, u32[]{:S(2)}) copy-start(f32[768]{0:T(1024)S(1)} %get-tuple-element.269) | copy-start | bytes 9220
  108.6 309.9 %copy-start.54 = (f32[768]{0:T(1024)}, f32[768]{0:T(1024)S(1)}, u32[]{:S(2)}) copy-start(f32[768]{0:T(1024)S(1)} %get-tuple-element.270) | copy-start | bytes 9220
  344.3 74.3 %copy-start.13 = (f32[576,768]{1,0:T(8,128)}, f32[576,768]{1,0:T(8,128)S(1)}, u32[]{:S(2)}) copy-start(f32[576,768]{1,0:T(8,128)S(1)} %get-tuple-element.382) | copy-start | bytes 5308420
  344.3 74.3 %copy-start.62 = (f32[576]{0:T(1024)}, f32[576]{0:T(1024)S(1)}, u32[]{:S(2)}) copy-start(f32[576]{0:T(1024)S(1)} %broadcast_multiply_fusion.12) | copy-start | bytes 6916
  345.5 73.1 %copy-start.64 = (f32[576]{0:T(1024)}, f32[576]{0:T(1024)S(1)}, u32[]{:S(2)}) copy-start(f32[576]{0:T(1024)S(1)} %add_rsqrt_fusion.2) | copy-start | bytes 6916
  699.6 223.9 %reduce-scatter.8.cloned.1.call-start = ((), (), s32[]{:S(2)}) async-start(), calls=%async_computation.9 | async-start | bytes 2433024 | tf_op jit(solution)/shard_map/reduce_scatter | solution.py:377
  704.1 344.6 %reduce-scatter.6.cloned.1.call-start = ((), (), s32[]{:S(2)}) async-start(), calls=%async_computation.8 | async-start | bytes 7299072 | tf_op jit(solution)/shard_map/reduce_scatter | solution.py:376
  715.0 475.1 %reduce-scatter.10.cloned.1.call-start = ((), (), s32[]{:S(2)}) async-start(), calls=%async_computation.10 | async-start | bytes 9732096 | tf_op jit(solution)/shard_map/reduce_scatter | solution.py:378
  729.7 602.6 %reduce-scatter.12.cloned.1.call-start = ((), (), s32[]{:S(2)}) async-start(), calls=%async_computation.11 | async-start | bytes 9732096 | tf_op jit(solution)/shard_map/reduce_scatter | solution.py:379
  (113 other events, 732.7 us)
Sparse Core Ops, SparseCore 0:
  11.5 62.8 all-gather.5
  77.9 52.9 all-gather.7
  133.8 62.5 all-gather.9
  199.1 62.4 all-gather.11
  699.7 118.0 all-reduce.5
  823.5 99.9 reduce-scatter.7
  930.7 117.9 reduce-scatter.5
  1055.2 134.8 reduce-scatter.9
  1197.6 134.6 reduce-scatter.11
where the time goes:
time: 1350 us; the launch traced here: 1340 us
  waiting for transfers between devices  568 us (42%)
  local copies, waits for them, and re-layouts  304 us (23%)
  matrix products  291 us (22%)
  blocking collectives  82.6 us (6%)
  other arithmetic  78.1 us (6%)
  between operations  15.9 us (1%)
    reduce_scatter x1, waiting for transfers between devices, shards(): lax.psum_scatter(totals[3], ('dp', 'fsdp'), scatter_dimension=0, tiled=True)  142 us
    reduce_scatter x1, waiting for transfers between devices, shards(): lax.psum_scatter(totals[2], ('dp', 'fsdp'), scatter_dimension=0, tiled=True)  141 us
    reduce_scatter x1, waiting for transfers between devices, shards(): lax.psum_scatter(totals[0], ('dp', 'fsdp'), scatter_dimension=0, tiled=True)  125 us
    reduce_scatter x1, waiting for transfers between devices, shards(): lax.psum_scatter(totals[1], ('dp', 'fsdp'), scatter_dimension=0, tiled=True)  103 us
    unnamed x10, waiting for transfers between devices  56.4 us
    add x2, local copies, waits for them, and re-layouts, backward_one_image(): left_part + right_part  51.1 us
    dot_general x2, matrix products, forward_image(): jnp.dot(normed_two, expand_w, preferred_element_type=jnp.float32)  45 us
    dot_general x8, matrix products, contract_rows(): lax.dot_general(left_rows, right_rows, (((0,), (0,)), ((), ())), preferre...  44.8 us
  transfers between devices with their start and end apart: 9, of which 5 were waited for; matrix products, arithmetic and copies ran while one was open for 24% of the time, Pallas kernels for 0%

commit v1 on v0

v1 whole, which is shorter than its diff:
```python
import math
import functools

import numpy as np
import jax
import jax.numpy as jnp
from jax import lax
from jax.experimental import pallas as pl
from jax.experimental.pallas import tpu as pltpu
from jax.sharding import PartitionSpec as P

D = 768
FF = 3072
HEADS = 24
HEAD_DIM = 32
WIN = 12
SIDE = 24
SHIFT = 6
TOK = SIDE * SIDE
WT = WIN * WIN
GROUPS = 3
GH = HEADS // GROUPS
GW = GH * HEAD_DIM
QL = GH * WT
SCALE = HEAD_DIM ** -0.5
MASKED = -1e30
EPS = 1e-5
F32 = jnp.float32
BF16 = jnp.bfloat16
VMEM_LIMIT = 62 << 20

NN = (((1,), (0,)), ((), ()))
NT = (((1,), (1,)), ((), ()))
TN = (((0,), (0,)), ((), ()))


def dot(a, b, dims=NN):
    return lax.dot_general(a, b, dims, preferred_element_type=F32)


def layout_constants():
    j = np.arange(WT)
    raster = np.zeros((4, WT), np.int32)
    label = np.zeros((4, WT), np.int32)
    for w in range(4):
        rr = (w // 2) * WIN + j // WIN
        rc = (w % 2) * WIN + j % WIN
        raster[w] = ((rr + SHIFT) % SIDE) * SIDE + (rc + SHIFT) % SIDE
        reg = lambda c: (c >= SIDE - WIN).astype(np.int32) + (c >= SIDE - SHIFT).astype(np.int32)
        label[w] = reg(rr) * 3 + reg(rc)
    perm = np.zeros((TOK, TOK), np.float32)
    perm[np.arange(TOK), raster.reshape(-1)] = 1.0
    raster_l = np.broadcast_to(raster[:, :, None], (4, WT, 128)).astype(np.int32)
    label_l = np.broadcast_to(label[:, :, None], (4, WT, 128)).astype(np.int32)
    label_q = np.broadcast_to(np.tile(label, (1, GH))[:, None, :], (4, 8, QL)).astype(np.int32)
    ext = 2 * WIN - 1
    target = np.full((4, WT), -1, np.int32)
    for p in range(4):
        r = j // WIN + (WIN - 1 if p // 2 == 0 else -1)
        s = j % WIN + (WIN - 1 if p % 2 == 0 else -1)
        ok = (r >= 0) & (s >= 0)
        target[p] = np.where(ok, r * ext + s, -1)
    target = np.broadcast_to(target.reshape(1, 4 * WT), (8, 4 * WT)).astype(np.int32)
    return perm, raster_l, label_l, label_q, target


PERM, RASTER_L, LABEL_L, LABEL_Q, TARGET = layout_constants()


def lane_iota(shape):
    return lax.broadcasted_iota(jnp.int32, shape, len(shape) - 1)


def stats(x):
    mean = jnp.mean(x, axis=-1, keepdims=True)
    center = x - mean
    var = jnp.mean(center * center, axis=-1, keepdims=True)
    inv = lax.rsqrt(var + EPS)
    return center * inv, inv


def head_stack(dst, x):
    lane = lane_iota(x.shape) // HEAD_DIM
    zero = jnp.zeros_like(x)
    for h in range(GH):
        dst[h * WT:(h + 1) * WT, :] = jnp.where(lane == h, x, zero)


def head_pick(o):
    lane = lane_iota((WT, GW)) // HEAD_DIM
    out = jnp.where(lane == 0, o[0:WT], 0.0)
    for h in range(1, GH):
        out = jnp.where(lane == h, o[h * WT:(h + 1) * WT], out)
    return out


def onehot(target_ref):
    ext = (2 * WIN - 1) ** 2
    t = lax.broadcasted_iota(jnp.int32, (ext, 4 * WT), 0)
    return (t == target_ref[0:1, :]).astype(F32)


def spread_bias(table_ref, target_ref, t4, bias, rowbuf):
    t4[...] = lax.dot_general(table_ref[...], onehot(target_ref), TN,
                              precision=lax.Precision.HIGHEST, preferred_element_type=F32) * (1.0 / SCALE)
    lane = lane_iota((1, QL))
    a_of = (lane % WT) // WIN
    lane16 = lane_iota((16, QL))
    c_of = lane16 % WIN
    for g in range(GROUPS):
        rows = []
        for p in range(4):
            acc = jnp.zeros((1, QL), F32)
            for h in range(GH):
                piece = t4[g * GH + h:g * GH + h + 1, p * WT:(p + 1) * WT]
                piece = jnp.concatenate([piece, jnp.zeros((1, QL - WT), F32)], axis=1)
                acc = acc + (pltpu.roll(piece, h * WT, axis=1) if h else piece)
            rows.append(acc)
        for s in range(2):
            for b in range(WIN):
                pos = pltpu.roll(rows[s], WIN * b, axis=1) if b else rows[s]
                neg = pltpu.roll(rows[2 + s], (WIN * b - WT) % QL, axis=1)
                rowbuf[s, b:b + 1, :] = jnp.where(a_of >= b, pos, neg)
        for d in range(WIN):
            pos = pltpu.roll(rowbuf[0], d, axis=1) if d else rowbuf[0]
            neg = pltpu.roll(rowbuf[1], (d - WIN) % QL, axis=1)
            both = jnp.where(c_of >= d, pos, neg)
            for n in range(9):
                bias[g * 9 + n, pl.ds(d, WIN, stride=WIN), :] = both[0:WIN, n * 128:(n + 1) * 128]


def fwd_kernel(counts, x, perm, raster, labk, labq, target, table, tm, sv,
               xp, normed, triple, pt, attended, mixed, n2,
               t4, bias, rowbuf, qs, st, lk):
    spread_bias(table, target, t4, bias, rowbuf)

    def ln1(i, _):
        b, w = i // 4, i % 4
        rows = pl.ds(pl.multiple_of(i * WT, WT), WT)
        pr = perm[pl.ds(pl.multiple_of(w * WT, WT), WT), :]
        xx = dot(pr, x[b])
        xp[rows, :] = xx.astype(BF16)
        hat, _i = stats(xx)
        normed[rows, :] = (hat * sv[0:1, :] + sv[1:2, :]).astype(BF16)
        return 0

    lax.fori_loop(0, 8, ln1, 0)

    for n in range(9):
        cols = pl.ds(n * 256, 256)
        r = dot(normed[...], tm[:, cols])
        if n < 3:
            r = r + sv[2:3, cols]
        if n >= 6:
            r = r + sv[3:4, pl.ds((n - 6) * 256, 256)]
        triple[:, cols] = r.astype(BF16)

    def attn(t, _):
        i, g = t // GROUPS, t % GROUPS
        b, w = i // 4, i % 4
        rows = pl.ds(pl.multiple_of(i * WT, WT), WT)
        col = lambda k: pl.ds(pl.multiple_of(k * D + g * GW, GW), GW)
        valid = raster[w] < counts[b]
        lk[...] = jnp.where(valid, labk[w], -1)
        head_stack(qs, triple[rows, col(0)])
        st[...] = dot(triple[rows, col(1)], qs[...], NT)
        for n in range(9):
            c = pl.ds(n * 128, 128)
            s = st[:, c] + bias[g * 9 + n]
            s = jnp.where(lk[...] == labq[w, 0:1, c], s, MASKED)
            m = jnp.max(s, axis=0, keepdims=True)
            e = jnp.exp((s - m) * SCALE)
            tot = jnp.sum(e, axis=0, keepdims=True)
            pt[t, :, c] = (e * (1.0 / tot)).astype(BF16)
        o = dot(pt[t], triple[rows, col(2)], TN)
        out = head_pick(o)
        vq = jnp.concatenate([valid, valid], axis=1)
        attended[rows, pl.ds(pl.multiple_of(g * GW, GW), GW)] = jnp.where(vq, out, 0.0).astype(BF16)
        return 0

    lax.fori_loop(0, 8 * GROUPS, attn, 0)

    for n in range(3):
        cols = pl.ds(n * 256, 256)
        r = dot(attended[...], tm[:, pl.ds(2304 + n * 256, 256)])
        mixed[:, cols] = xp[:, cols].astype(F32) + r + sv[4:5, cols]

    def ln2(i, _):
        rows = pl.ds(pl.multiple_of(i * WT, WT), WT)
        hat, _i = stats(mixed[rows, :])
        n2[rows, :] = (hat * sv[5:6, :] + sv[6:7, :]).astype(BF16)
        return 0

    lax.fori_loop(0, 8, ln2, 0)


def call(kernel, outs, scratch, ins, smem=0, name=None):
    specs = [pl.BlockSpec(memory_space=pltpu.SMEM)] * smem + [pl.BlockSpec(memory_space=pltpu.VMEM)] * (len(ins) - smem)
    return pl.pallas_call(
        kernel,
        out_shape=[jax.ShapeDtypeStruct(s, d) for s, d in outs],
        in_specs=specs,
        out_specs=[pl.BlockSpec(memory_space=pltpu.VMEM)] * len(outs),
        scratch_shapes=scratch,
        name=name,
        compiler_params=pltpu.CompilerParams(vmem_limit_bytes=VMEM_LIMIT),
    )(*ins)


def forward(counts, x, table, tm, sv):
    rows = 2 * TOK
    return call(
        fwd_kernel,
        [((rows, D), BF16), ((rows, D), BF16), ((rows, 3 * D), BF16), ((8 * GROUPS, WT, QL), BF16),
         ((rows, D), BF16), ((rows, D), F32), ((rows, D), BF16)],
        [pltpu.VMEM((HEADS, 4 * WT), F32), pltpu.VMEM((GROUPS * 9, WT, 128), F32), pltpu.VMEM((2, 16, QL), F32),
         pltpu.VMEM((QL, GW), BF16), pltpu.VMEM((WT, QL), F32), pltpu.VMEM((WT, 128), jnp.int32)],
        [counts, x, jnp.asarray(PERM, BF16), jnp.asarray(RASTER_L), jnp.asarray(LABEL_L), jnp.asarray(LABEL_Q),
         jnp.asarray(TARGET), table, tm, sv], smem=1, name="fwd")


ERF_SLOPE = 0.35
ERF_FIT = (0.19434814435164116, 0.235843067071591, -0.008625688056468914, 0.6849613674275746, -0.6811631064960405, 0.7727015621272543, -0.19806535099226122)


def gelu_pair(v):
    e = jnp.exp(v * v * -0.5)
    t = 1.0 / (1.0 + jnp.abs(v) * (ERF_SLOPE * math.sqrt(0.5)))
    poly = jnp.full_like(t, 0.5 * ERF_FIT[-1])
    for c in ERF_FIT[-2::-1]:
        poly = poly * t + 0.5 * c
    tail = poly * t * e
    cdf = jnp.where(v >= 0, 1.0 - tail, tail)
    return v * cdf, cdf + v * e * (1.0 / math.sqrt(2.0 * math.pi))


def ffn_kernel(do, perm, unperm, n2, mixed, ew, rw, eb, sv,
               out, dop, dre, dex, dn2, deb, drb,
               act, hlow, hs, ds, n2t, part):
    def permute(i, _):
        b, w = i // 4, i % 4
        rows = pl.ds(pl.multiple_of(i * WT, WT), WT)
        dop[rows, :] = dot(perm[pl.ds(pl.multiple_of(w * WT, WT), WT), :], do[b]).astype(BF16)
        return 0

    lax.fori_loop(0, 8, permute, 0)
    n2t[...] = n2[...].T
    drb[...] = jnp.sum(dop[...].astype(F32), axis=0, keepdims=True)

    def chunk(j, _):
        c = pl.ds(pl.multiple_of(j * 256, 256), 256)
        hs[...] = dot(n2[...], ew[:, c])
        ds[...] = dot(dop[...], rw[c, :], NT)
        bias = eb[0:1, c]
        total = jnp.zeros((8, 256), F32)
        for r in range(18):
            rr = pl.ds(r * 64, 64)
            a, s = gelu_pair(hs[rr, :] + bias)
            act[rr, c] = a.astype(BF16)
            hg = ds[rr, :] * s
            for q in range(8):
                total = total + hg[q * 8:(q + 1) * 8]
            hlow[rr, c] = hg.astype(BF16)
        deb[0:1, c] = jnp.sum(total, axis=0, keepdims=True)
        dre[c, :] = dot(act[:, c], dop[...], TN).astype(BF16)
        dex[:, c] = dot(n2t[...], hlow[:, c]).astype(BF16)
        return 0

    lax.fori_loop(0, FF // 256, chunk, 0)

    for n in range(3):
        c = pl.ds(n * 256, 256)
        part[:, c] = (mixed[:, c] + dot(act[...], rw[:, c]) + sv[7:8, c]).astype(BF16)
        dn2[:, c] = dot(hlow[...], ew[c, :], NT)
    for b in range(2):
        for m in range(4):
            rows = pl.ds(m * WT, WT)
            out[b, rows, :] = dot(unperm[rows, :], part[b * TOK:(b + 1) * TOK, :]).astype(BF16)


def ffn(do, n2, mixed, ew, rw, eb, sv):
    rows = 2 * TOK
    return call(
        ffn_kernel,
        [((2, TOK, D), BF16), ((rows, D), BF16), ((FF, D), BF16), ((D, FF), BF16), ((rows, D), F32), ((1, FF), F32),
         ((1, D), F32)],
        [pltpu.VMEM((rows, FF), BF16), pltpu.VMEM((rows, FF), BF16), pltpu.VMEM((rows, 256), F32),
         pltpu.VMEM((rows, 256), F32), pltpu.VMEM((D, rows), BF16), pltpu.VMEM((rows, D), BF16)],
        [do, jnp.asarray(PERM, BF16), jnp.asarray(PERM.T, BF16), n2, mixed, ew, rw, eb, sv], name="ffn")


def bwd_kernel(counts, unperm, raster, target, mixed, dn2, dop, attended, triple, pt, normed, xp, tm, sv,
               dx, dtm, sg, dtab,
               mg, ml, datt, dtri, bgrad, qs, dos, st, raw, stage, attt, accbuf, t4):
    sgrow = lambda k, v: sg.__setitem__((pl.ds(k, 1), slice(None)), v)

    def norm_back(hat, inv, gain, grad):
        scaled = grad * gain
        return inv * (scaled - jnp.mean(scaled, axis=-1, keepdims=True)
                      - hat * jnp.mean(scaled * hat, axis=-1, keepdims=True))

    sg[...] = jnp.zeros_like(sg)

    def ln2b(i, _):
        rows = pl.ds(pl.multiple_of(i * WT, WT), WT)
        hat, inv = stats(mixed[rows, :])
        g = dn2[rows, :]
        sg[5:6, :] += jnp.sum(g * hat, axis=0, keepdims=True)
        sg[6:7, :] += jnp.sum(g, axis=0, keepdims=True)
        m = dop[rows, :].astype(F32) + norm_back(hat, inv, sv[5:6, :], g)
        sg[4:5, :] += jnp.sum(m, axis=0, keepdims=True)
        mg[rows, :] = m
        ml[rows, :] = m.astype(BF16)
        return 0

    lax.fori_loop(0, 8, ln2b, 0)
    attt[...] = attended[...].T
    for n in range(3):
        c = pl.ds(n * 256, 256)
        dtm[:, pl.ds(2304 + n * 256, 256)] = dot(attt[...], ml[:, c]).astype(BF16)
        datt[:, c] = dot(ml[...], tm[c, 2304:3072], NT).astype(BF16)

    bgrad[...] = jnp.zeros_like(bgrad)

    def attn(t, _):
        i, g = t // GROUPS, t % GROUPS
        b, w = i // 4, i % 4
        rows = pl.ds(pl.multiple_of(i * WT, WT), WT)
        col = lambda k: pl.ds(pl.multiple_of(k * D + g * GW, GW), GW)
        valid = raster[w] < counts[b]
        vq = jnp.concatenate([valid, valid], axis=1)
        da = datt[rows, pl.ds(pl.multiple_of(g * GW, GW), GW)]
        da = jnp.where(vq, da.astype(F32), 0.0).astype(BF16)
        head_stack(qs, triple[rows, col(0)])
        head_stack(dos, da)
        st[...] = dot(triple[rows, col(2)], dos[...], NT)
        for n in range(9):
            c = pl.ds(n * 128, 128)
            p = pt[t, :, c].astype(F32)
            d = st[:, c]
            inner = jnp.sum(p * d, axis=0, keepdims=True)
            s = p * (d - inner)
            bgrad[g * 9 + n] += s
            raw[:, c] = (s * SCALE).astype(BF16)
        dtri[rows, col(2)] = dot(pt[t], dos[...]).astype(BF16)
        dtri[rows, col(1)] = dot(raw[...], qs[...]).astype(BF16)
        dtri[rows, col(0)] = head_pick(dot(raw[...], triple[rows, col(0 + 1)], TN)).astype(BF16)
        return 0

    lax.fori_loop(0, 8 * GROUPS, attn, 0)
    gather_bias(bgrad, accbuf, t4, target, dtab)

    attt[...] = normed[...].T
    for n in range(9):
        c = pl.ds(n * 256, 256)
        if n < 3 or n >= 6:
            k, o = (2, n * 256) if n < 3 else (3, (n - 6) * 256)
            sg[k:k + 1, o:o + 256] = jnp.sum(dtri[:, c].astype(F32), axis=0, keepdims=True)
        dtm[:, c] = dot(attt[...], dtri[:, c]).astype(BF16)
    for n in range(3):
        c = pl.ds(n * 256, 256)
        stage[:, c] = dot(dtri[...], tm[c, 0:2304], NT)

    def ln1b(i, _):
        rows = pl.ds(pl.multiple_of(i * WT, WT), WT)
        hat, inv = stats(xp[rows, :].astype(F32))
        g = stage[rows, :]
        sg[0:1, :] += jnp.sum(g * hat, axis=0, keepdims=True)
        sg[1:2, :] += jnp.sum(g, axis=0, keepdims=True)
        m = mg[rows, :] + norm_back(hat, inv, sv[0:1, :], g)
        ml[rows, :] = m.astype(BF16)
        return 0

    lax.fori_loop(0, 8, ln1b, 0)
    for b in range(2):
        for m in range(4):
            rows = pl.ds(m * WT, WT)
            dx[b, rows, :] = dot(unperm[rows, :], ml[b * TOK:(b + 1) * TOK, :]).astype(BF16)


def gather_bias(bgrad, accbuf, t4, target, dtab):
    lane = lane_iota((1, QL))
    a_of = (lane % WT) // WIN
    c_of = lane_iota((WIN, QL)) % WIN
    for g in range(GROUPS):
        pos = jnp.zeros((WIN, QL), F32)
        neg = jnp.zeros((WIN, QL), F32)
        for d in range(WIN):
            r = jnp.concatenate([bgrad[g * 9 + n, pl.ds(d, WIN, stride=WIN), :] for n in range(9)], axis=1)
            p = jnp.where(c_of >= d, r, 0.0)
            pos = pos + (pltpu.roll(p, QL - d, axis=1) if d else p)
            if d:
                neg = neg + pltpu.roll(jnp.where(c_of < d, r, 0.0), WIN - d, axis=1)
        accbuf[0, 0:WIN, :] = pos
        accbuf[1, 0:WIN, :] = neg
        for s in range(2):
            pp = jnp.zeros((1, QL), F32)
            nn = jnp.zeros((1, QL), F32)
            for b in range(WIN):
                r = accbuf[s, b:b + 1, :]
                p = jnp.where(a_of >= b, r, 0.0)
                pp = pp + (pltpu.roll(p, QL - WIN * b, axis=1) if b else p)
                if b:
                    nn = nn + pltpu.roll(jnp.where(a_of < b, r, 0.0), WT - WIN * b, axis=1)
            for part, row in ((s, pp), (2 + s, nn)):
                for h in range(GH):
                    moved = pltpu.roll(row, QL - h * WT, axis=1) if h else row
                    t4[g * GH + h:g * GH + h + 1, part * WT:(part + 1) * WT] = moved[:, 0:WT]
    dtab[...] = t4[...]


def backward(counts, mixed, dn2, dop, attended, triple, pt, normed, xp, tm, sv):
    rows = 2 * TOK
    return call(
        bwd_kernel,
        [((2, TOK, D), BF16), ((D, 4 * D), BF16), ((8, D), F32), ((HEADS, 4 * WT), F32)],
        [pltpu.VMEM((rows, D), F32), pltpu.VMEM((rows, D), BF16), pltpu.VMEM((rows, D), BF16),
         pltpu.VMEM((rows, 3 * D), BF16), pltpu.VMEM((GROUPS * 9, WT, 128), F32), pltpu.VMEM((QL, GW), BF16),
         pltpu.VMEM((QL, GW), BF16), pltpu.VMEM((WT, QL), F32), pltpu.VMEM((WT, QL), BF16),
         pltpu.VMEM((rows, D), F32), pltpu.VMEM((D, rows), BF16),
         pltpu.VMEM((2, 16, QL), F32), pltpu.VMEM((HEADS, 4 * WT), F32)],
        [counts, jnp.asarray(PERM.T, BF16), jnp.asarray(RASTER_L), jnp.asarray(TARGET), mixed, dn2, dop, attended,
         triple, pt, normed, xp, tm, sv], smem=1, name="bwd")


def table_kernel(target, t4, table):
    table[...] = lax.dot_general(onehot(target), t4[...], NT, precision=lax.Precision.HIGHEST,
                                 preferred_element_type=F32)


AXES = ("dp", "fsdp")
MESH = pl.DeviceIdType.MESH


class Place:
    def __init__(self, dims):
        self.nz, self.ny, self.nx = dims
        f = lax.axis_index("fsdp")
        self.z = lax.axis_index("dp")
        self.c = lax.rem(f, 2)
        self.x = lax.rem(f // 2, self.nx)
        self.y = f // (2 * self.nx)

    def size(self, axis):
        return {"z": self.nz, "y": self.ny, "x": self.nx, "c": 2}[axis]

    def at(self, axis):
        return {"z": self.z, "y": self.y, "x": self.x, "c": self.c}[axis]

    def step(self, axis, k):
        n = self.size(axis)
        return lax.rem(self.at(axis) + k, n)

    def device(self, axis, k):
        p = {a: (self.step(a, k) if a == axis else self.at(a)) for a in "zyxc"}
        return (p["z"], (p["y"] * self.nx + p["x"]) * 2 + p["c"])

    def greet(self):
        barrier = pltpu.get_barrier_semaphore()
        total = 0
        for axis in "czyx":
            for k in range(1, self.size(axis)):
                pl.semaphore_signal(barrier, inc=1, device_id=self.device(axis, k), device_id_type=MESH)
                total += 1
        pl.semaphore_wait(barrier, total)


def mesh_dims(mesh):
    chips = mesh.shape["fsdp"] // 2
    ny = max(n for n in range(1, chips + 1) if n * n <= chips and chips % n == 0)
    return mesh.shape["dp"], ny, chips // ny


class Sems:
    def __init__(self, send, recv):
        self.send, self.recv, self.used = send, recv, 0

    def take(self):
        self.used += 1
        return self.send.at[self.used - 1], self.recv.at[self.used - 1]


class Swap:
    def __init__(self, place, sems, axis, src, dst, from_slot):
        self.copies = []
        for k in range(1, place.size(axis)):
            s, r = sems.take()
            out = pltpu.make_async_remote_copy(src_ref=src(k), dst_ref=dst(k), send_sem=s, recv_sem=r,
                                               device_id=place.device(axis, k), device_id_type=MESH)
            back = pltpu.make_async_remote_copy(src_ref=from_slot(k), dst_ref=from_slot(k), send_sem=s, recv_sem=r,
                                                device_id=place.device(axis, k), device_id_type=MESH)
            self.copies.append((out, back))

    def start(self):
        for out, _ in self.copies:
            out.start()

    def arrive(self):
        for _, back in self.copies:
            back.wait_recv()

    def done(self):
        for out, _ in self.copies:
            out.wait_send()


def cols_at(c, half, lo, width):
    return pl.ds(pl.multiple_of(c * half + lo, 128), width)


def gather_chain(place, sems, ref, order, block):
    z, y, x = place.z, place.y, place.x
    first, second = order
    own = lambda zz, yy, xx: ref.at[(zz, yy, xx) + block(place.c)]
    every = slice(None)
    chain = [Swap(place, sems, "z", lambda k: own(z, y, x), lambda k: own(z, y, x),
                  lambda k: own(place.step("z", place.nz - k), y, x))]
    back = lambda a, k: place.step(a, place.size(a) - k)
    if first == "x":
        chain.append(Swap(place, sems, "x", lambda k: own(every, y, x), lambda k: own(every, y, x),
                          lambda k: own(every, y, back("x", k))))
        chain.append(Swap(place, sems, "y", lambda k: own(every, y, every), lambda k: own(every, y, every),
                          lambda k: own(every, back("y", k), every)))
    else:
        chain.append(Swap(place, sems, "y", lambda k: own(every, y, x), lambda k: own(every, y, x),
                          lambda k: own(every, back("y", k), x)))
        chain.append(Swap(place, sems, "x", lambda k: own(every, every, x), lambda k: own(every, every, x),
                          lambda k: own(every, every, back("x", k))))
    mine = lambda k: ref.at[(every, every, every) + block(place.c)]
    other = lambda k: ref.at[(every, every, every) + block(1 - place.c)]
    chain.append(Swap(place, sems, "c", mine, mine, other))
    return chain


def wide_block(lo, width, r=None):
    def block(c):
        return (slice(None) if r is None else r, cols_at(c, 1536, lo, width))
    return block


def tall_block(lo, rows):
    def block(c):
        return (pl.ds(lo, rows), cols_at(c, 384, 0, 384))
    return block


def gather_pieces(place, sems, tm, ew, rw, sb):
    both = lambda ref, make, parts: [gather_chain(place, sems, ref, o, make(*p)) for o, p in zip(("xy", "yx"), parts)]
    small = gather_chain(place, sems, sb, "xy", lambda c: (c,))
    pieces = []
    for ref in (tm, ew):
        for p in range(2):
            lo = p * 768
            pieces.append(both(ref, wide_block, ((lo, 384), (lo + 384, 384))))
    rows = rw.shape[3]
    for p in range(2):
        lo = p * rows // 2
        pieces.append(both(rw, tall_block, ((lo, rows // 4), (lo + rows // 4, rows // 4))))
    pieces[0].append(small)
    return pieces


def run_chains(pieces):
    depth = 4
    for t in range(len(pieces) + depth):
        for p in range(max(0, t - depth), min(t, len(pieces) - 1) + 1):
            s = t - p
            for chain in pieces[p]:
                if s > 0:
                    chain[s - 1].arrive()
                if s < depth:
                    chain[s].start()
    for piece in pieces:
        for chain in piece:
            for swap in chain:
                swap.done()


def place_small(sb, sv, eb, lanes, wide):
    nz, ny, nx = sb.shape[:3]
    for out, row0, width, total in ((sv, 0, lanes, D), (eb, 8, wide, FF)):
        tiles = [jnp.zeros((8, 128), F32) for _ in range(total // 128)]
        lane = lane_iota((8, 128))
        n = 0
        for q in range(nz * ny * nx):
            for c in range(2):
                blk = sb[q // (ny * nx), (q // nx) % ny, q % nx, c, row0:row0 + 8, :]
                tile, off = divmod(n * width, 128)
                moved = pltpu.roll(blk, off, axis=1) if off else blk
                end = off + width
                tiles[tile] = jnp.where((lane >= off) & (lane < min(end, 128)), moved, tiles[tile])
                if end > 128:
                    tiles[tile + 1] = jnp.where(lane < end - 128, moved, tiles[tile + 1])
                n += 1
        out[...] = jnp.concatenate(tiles, axis=1)


def own_blocks(place, sems, stage_tm, stage_ew, stage_rw, mt, me, mr):
    swaps = []
    for ref, stage, half in ((mt, stage_tm, 1536), (me, stage_ew, 1536), (mr, stage_rw, 384)):
        r = ref.shape[0]
        mine = pl.ds(pl.multiple_of(place.c * r, 8), r)
        theirs = pl.ds(pl.multiple_of((1 - place.c) * r, 8), r)
        swaps.append(Swap(place, sems, "c", lambda k, ref=ref, half=half: ref.at[:, cols_at(1 - place.c, half, 0, half)],
                          lambda k, stage=stage, mine=mine: stage.at[mine, :],
                          lambda k, stage=stage, theirs=theirs: stage.at[theirs, :]))
    return swaps


def gather_kernel(dims, mt, me, mr, small, tm, ew, rw, sv, eb, sb, st_t, st_e, st_r, send, recv):
    place = Place(dims)
    sems = Sems(send, recv)
    place.greet()
    first = own_blocks(place, sems, st_t, st_e, st_r, mt, me, mr)
    for s in first:
        s.start()
    z, y, x, c = place.z, place.y, place.x, place.c
    sb[z, y, x, c] = small[...].astype(BF16).astype(F32)
    for s, ref, stage, full, half in zip(first, (mt, me, mr), (st_t, st_e, st_r), (tm, ew, rw), (1536, 1536, 384)):
        r = ref.shape[0]
        stage[pl.ds(pl.multiple_of(c * r, 8), r), :] = ref[:, cols_at(c, half, 0, half)]
        s.arrive()
        full[z, y, x, :, cols_at(c, half, 0, half)] = stage[...].astype(BF16)
    run_chains(gather_pieces(place, sems, tm, ew, rw, sb))
    for s in first:
        s.done()
    place_small(sb, sv, eb, D // (2 * dims[0] * dims[1] * dims[2]), FF // (2 * dims[0] * dims[1] * dims[2]))


def gather_weights(dims, mt, me, mr, small):
    nz, ny, nx = dims
    r, rr = mt.shape[0], mr.shape[0]
    n = 3 + 13 * (nz + ny + nx - 2)
    return pl.pallas_call(
        functools.partial(gather_kernel, dims),
        out_shape=[jax.ShapeDtypeStruct((nz, ny, nx, 2 * r, 4 * D), BF16), jax.ShapeDtypeStruct((nz, ny, nx, 2 * r, FF), BF16),
                   jax.ShapeDtypeStruct((nz, ny, nx, 2 * rr, D), BF16), jax.ShapeDtypeStruct((8, D), F32),
                   jax.ShapeDtypeStruct((8, FF), F32)],
        in_specs=[pl.BlockSpec(memory_space=pltpu.VMEM)] * 4,
        out_specs=[pl.BlockSpec(memory_space=pltpu.VMEM)] * 5,
        scratch_shapes=[pltpu.VMEM((nz, ny, nx, 2, 16, 128), F32), pltpu.VMEM((2 * r, 1536), F32),
                        pltpu.VMEM((2 * r, 1536), F32), pltpu.VMEM((2 * rr, 384), F32),
                        pltpu.SemaphoreType.DMA((n,)), pltpu.SemaphoreType.DMA((n,))],
        name="gather",
        compiler_params=pltpu.CompilerParams(vmem_limit_bytes=VMEM_LIMIT, collective_id=0, has_side_effects=True),
    )(mt, me, mr, small)


def scatter_chain(place, sems, g, recv0, recv1, recv2, recv3, out, order, part):
    z, y, x, c = place.z, place.y, place.x, place.c
    every = slice(None)
    lo_row, n_row, half, lo, width = part
    rows = pl.ds(lo_row, n_row)
    mine, other = cols_at(c, half, lo, width), cols_at(1 - c, half, lo, width)
    first, second = order
    place_of = {"z": z, "y": y, "x": x}

    def pick(a, v, b=None, w=None):
        sel = {"z": every, "y": every, "x": every}
        sel[a] = v
        if b:
            sel[b] = w
        return (sel["z"], sel["y"], sel["x"])

    steps = []
    swap = Swap(place, sems, "c", lambda k: g.at[every, every, every, rows, other], lambda k: recv0, lambda k: recv0)

    def add0():
        recv0[...] = (recv0[...].astype(F32) + g[:, :, :, rows, mine].astype(F32)).astype(BF16)

    steps.append((swap, add0))
    n1 = place.size(first)
    slot = lambda a, k: place.size(a) - 1 - k
    swap = Swap(place, sems, first, lambda k: recv0.at[pick(first, place.step(first, k))], lambda k: recv1.at[k - 1],
                lambda k: recv1.at[k - 1])

    def add1():
        s = recv0[pick(first, place_of[first])].astype(F32)
        for k in range(n1 - 1):
            s = s + recv1[k].astype(F32)
        recv1[0] = s.astype(BF16)

    steps.append((swap, add1))
    n2 = place.size(second)
    swap = Swap(place, sems, second, lambda k: recv1.at[(0, every, place.step(second, k))], lambda k: recv2.at[k - 1],
                lambda k: recv2.at[k - 1])

    def add2():
        s = recv1[(0, every, place_of[second])].astype(F32)
        for k in range(n2 - 1):
            s = s + recv2[k].astype(F32)
        recv2[0] = s.astype(BF16)

    steps.append((swap, add2))
    swap = Swap(place, sems, "z", lambda k: recv2.at[0, place.step("z", k)], lambda k: recv3.at[k - 1],
                lambda k: recv3.at[k - 1])
    final = recv3.shape[0]

    return steps, swap


def scatter_kernel(dims, dtm, dex, dre, sg, deb, t4, otm, oex, ore, osg, oeb, ot4, *scratch):
    place = Place(dims)
    nz, ny, nx = dims
    send, recv = scratch[-2:]
    sems = Sems(send, recv)
    place.greet()
    bufs = list(scratch[:-2])
    z, y, x, c = place.z, place.y, place.x, place.c
    every = slice(None)
    pieces, finals = [], []

    def piece(g, out, order, part):
        recv0, recv1, recv2, recv3, fin = bufs.pop(0), bufs.pop(0), bufs.pop(0), bufs.pop(0), bufs.pop(0)
        steps, zswap = scatter_chain(place, sems, g, recv0, recv1, recv2, recv3, out, order, part)
        lo_row, n_row, half, lo, width = part
        r = out.shape[0]

        def add3():
            s = recv2[0, z].astype(F32)
            for k in range(nz - 1):
                s = s + recv3[k].astype(F32)
            fin[...] = s

        steps.append((zswap, add3))
        return steps, fin

    def small_chain(buf, slots):
        steps = []
        for i, a in enumerate("cyxz"):
            n = place.size(a)
            base = sum(place.size(b) for b in "cyxz"[:i])
            me = base + place.at(a)
            swap = Swap(place, sems, a, lambda k, me=me: slots.at[me], lambda k, me=me: slots.at[me],
                        lambda k, base=base, n=n, a=a: slots.at[base + place.step(a, n - k)])

            def add(base=base, n=n, i=i):
                s = slots[base]
                for k in range(1, n):
                    s = s + slots[base + k]
                if i < 3:
                    b = "cyxz"[i + 1]
                    slots[base + n + place.at(b)] = s
                else:
                    buf[...] = s

            steps.append((swap, add))
        return steps

    buf, slots = bufs.pop(0), bufs.pop(0)
    slots[c] = jnp.zeros_like(buf)
    slots[c, 0:8, :] = sg[...]
    for k in range(4):
        slots[c, 8 + k:9 + k, :] = deb[0:1, k * D:(k + 1) * D]
    slots[c, 16:40, 0:4 * WT] = t4[...]

    last = []
    chains = []
    for g, out in ((dtm, otm), (dex, oex)):
        for p in range(2):
            pair = []
            for order, lo in (("yx", p * 768), ("xy", p * 768 + 384)):
                part = (0, g.shape[3], 1536, lo, 384)
                steps, fin = piece(g, out, order, part)
                pair.append(steps)
                last.append((out, fin, part))
            chains.append(pair)
    rr = dre.shape[3]
    for p in range(2):
        pair = []
        for order, lo in (("yx", p * rr // 2), ("xy", p * rr // 2 + rr // 4)):
            part = (lo, rr // 4, 384, 0, 384)
            steps, fin = piece(dre, ore, order, part)
            pair.append(steps)
            last.append((ore, fin, part))
        chains.append(pair)
    chains.append([small_chain(buf, slots)])
    depth = 4
    for t in range(len(chains) + depth):
        for p in range(max(0, t - depth), min(t, len(chains) - 1) + 1):
            s = t - p
            for steps in chains[p]:
                if s > 0:
                    steps[s - 1][0].arrive()
                    steps[s - 1][1]()
                if s < depth:
                    steps[s][0].start()
    for pair in chains:
        for steps in pair:
            for swap, _ in steps:
                swap.done()
    ends = []
    for out, fin, (lo_row, n_row, half, lo, width) in last:
        r = out.shape[0]
        if n_row == 2 * r:
            src = fin.at[pl.ds(pl.multiple_of((1 - c) * r, 8), r), :]
            dst = out.at[:, cols_at(c, half, lo, width)]
            back = out.at[:, cols_at(1 - c, half, lo, width)]
            out[:, cols_at(c, half, lo, width)] = fin[pl.ds(pl.multiple_of(c * r, 8), r), :]
            ends.append(Swap(place, sems, "c", lambda k, src=src: src, lambda k, dst=dst: dst, lambda k, back=back: back))
    tall = [(fin, part) for out, fin, part in last if out is ore]
    full = bufs.pop(0)
    for fin, (lo_row, n_row, half, lo, width) in tall:
        full[lo_row:lo_row + n_row, :] = fin[...]
    r = ore.shape[0]
    ore[:, cols_at(c, 384, 0, 384)] = full[pl.ds(pl.multiple_of(c * r, 8), r), :]
    ends.append(Swap(place, sems, "c", lambda k: full.at[pl.ds(pl.multiple_of((1 - c) * r, 8), r), :],
                     lambda k: ore.at[:, cols_at(c, 384, 0, 384)], lambda k: ore.at[:, cols_at(1 - c, 384, 0, 384)]))
    for e in ends:
        e.start()
    dev = z * (2 * ny * nx) + (y * nx + x) * 2 + c
    lanes = osg.shape[1]
    shift = lax.rem(D - dev * lanes, D)
    osg[...] = pltpu.roll(buf[0:8, :], shift, axis=1)[:, 0:lanes]
    wide = oeb.shape[1]
    per = D // wide
    row = buf[pl.ds(8 + dev // per, 1), :]
    oeb[...] = pltpu.roll(row, lax.rem(D - lax.rem(dev, per) * wide, D), axis=1)[:, 0:wide]
    ot4[...] = buf[16:40, 0:4 * WT]
    for e in ends:
        e.arrive()
        e.done()


def scatter_grads(dims, dtm, dex, dre, sg, deb, t4):
    nz, ny, nx = dims
    ndev = 2 * nz * ny * nx
    r, rr = D // ndev, FF // ndev
    scratch = [pltpu.VMEM((40, D), F32), pltpu.VMEM((2 + nz + ny + nx, 40, D), F32)]
    for i, (n_row, width) in enumerate([(2 * r, 384)] * 8 + [(2 * rr // 4, 384)] * 4):
        order = "xy" if i % 2 else "yx"
        n1, n2 = (ny, nx) if order == "yx" else (nx, ny)
        scratch += [pltpu.VMEM((nz, ny, nx, n_row, width), BF16), pltpu.VMEM((n1 - 1, nz, n2, n_row, width), BF16),
                    pltpu.VMEM((n2 - 1, nz, n_row, width), BF16), pltpu.VMEM((nz - 1, n_row, width), BF16),
                    pltpu.VMEM((n_row, width), F32)]
    n = 13 * (1 + nz + ny + nx - 3) + 9
    scratch += [pltpu.VMEM((2 * rr, 384), F32),
                pltpu.SemaphoreType.DMA((n,)), pltpu.SemaphoreType.DMA((n,))]
    return pl.pallas_call(
        functools.partial(scatter_kernel, dims),
        out_shape=[jax.ShapeDtypeStruct((r, 4 * D), F32), jax.ShapeDtypeStruct((r, FF), F32),
                   jax.ShapeDtypeStruct((rr, D), F32), jax.ShapeDtypeStruct((8, r), F32),
                   jax.ShapeDtypeStruct((1, rr), F32), jax.ShapeDtypeStruct((HEADS, 4 * WT), F32)],
        in_specs=[pl.BlockSpec(memory_space=pltpu.VMEM)] * 6,
        out_specs=[pl.BlockSpec(memory_space=pltpu.VMEM)] * 6,
        scratch_shapes=scratch,
        name="scatter",
        compiler_params=pltpu.CompilerParams(vmem_limit_bytes=VMEM_LIMIT, collective_id=1, has_side_effects=True),
    )(dtm.reshape(nz, ny, nx, 2 * r, 4 * D), dex.reshape(nz, ny, nx, 2 * r, FF), dre.reshape(nz, ny, nx, 2 * rr, D),
      sg, deb, t4)


def shards(dims, block_input, valid_counts, output_cotangent, triple_weight, merge_weight, expand_weight, reduce_weight,
           first_gain, first_shift, query_bias, value_bias, merge_bias, second_gain, second_shift, expand_bias,
           reduce_bias, position_table):
    x = block_input[:, 0]
    do = output_cotangent[:, 0]
    counts = valid_counts[:, 0]
    small = jnp.stack([first_gain, first_shift, query_bias, value_bias, merge_bias, second_gain, second_shift,
                       reduce_bias])
    tm_own = jnp.concatenate([triple_weight, merge_weight], axis=1)
    near = triple_weight.shape[0] % 8 == 0
    if near:
        block = jnp.zeros((16, 128), F32).at[:8, :small.shape[1]].set(small)
        block = block.at[8, :expand_bias.shape[0]].set(expand_bias)
        tm, ew, rw, sv, eb = gather_weights(dims, tm_own, expand_weight, reduce_weight, block)
        tm, ew, rw = tm.reshape(D, 4 * D), ew.reshape(D, FF), rw.reshape(FF, D)
    else:
        gather = lambda v, axis: lax.all_gather(v.astype(BF16), AXES, axis=axis, tiled=True)
        tm, ew, rw = gather(tm_own, 0), gather(expand_weight, 0), gather(reduce_weight, 0)
        sv, eb = gather(small, 1).astype(F32), gather(expand_bias, 0).astype(F32)[None]
    xp, normed, triple, pt, attended, mixed, n2 = forward(counts, x, position_table, tm, sv)
    out, dop, dre, dex, dn2, deb, drb = ffn(do, n2, mixed, ew, rw, eb, sv)
    dx, dtm, sg, t4 = backward(counts, mixed, dn2, dop, attended, triple, pt, normed, xp, tm, sv)
    sg = jnp.concatenate([sg[:7], drb])
    if near:
        otm, oex, ore, osg, oeb, ot4 = scatter_grads(dims, dtm, dex, dre, sg, deb, t4)
        oeb = oeb[0]
    else:
        scatter = lambda v, axis: lax.psum_scatter(v.astype(F32), AXES, scatter_dimension=axis, tiled=True)
        otm, oex, ore, osg, oeb = scatter(dtm, 0), scatter(dex, 0), scatter(dre, 0), scatter(sg, 1), scatter(deb[0], 0)
        ot4 = lax.psum(t4, AXES)
    table = call(table_kernel, [(((2 * WIN - 1) ** 2, HEADS), F32)], [], [jnp.asarray(TARGET), ot4], name="table")[0]
    return (out[:, None], dx[:, None], otm[:, :2304], otm[:, 2304:], oex, ore,
            osg[0], osg[1], osg[2], osg[3], osg[4], osg[5], osg[6], oeb, osg[7], table)


def solution(mesh):
    image = P(None, AXES, None, None)
    rows = P(AXES, None)
    vec = P(AXES)
    return jax.shard_map(
        functools.partial(shards, mesh_dims(mesh)), mesh=mesh,
        in_specs=(image, P(None, AXES), image) + (rows,) * 4 + (vec,) * 9 + (P(),),
        out_specs=(image, image) + (rows,) * 4 + (vec,) * 9 + (P(),),
        check_vma=False)
```

time: 1350 us -> 393 us (0.29)
  waiting for transfers between devices: 568 us -> 0 us
  Pallas kernels: 0 us -> 370 us
  matrix products: 291 us -> 0 us
  local copies, waits for them, and re-layouts: 304 us -> 14.2 us
  blocking collectives: 82.6 us -> 0 us
  other arithmetic: 78.1 us -> 3.06 us
  between operations: 15.9 us -> 0.92 us
    reduce_scatter x4 -> x0, waiting for transfers between devices: 512 us -> none  [the longest x1 142 us: shards(): lax.psum_scatter(totals[3], ('dp', 'fsdp'), scatter_dimension=0, tiled=True)]
    pallas_call x0 -> x6, Pallas kernels: none -> 370 us  [the longest x4 184 us: call(): pl.pallas_call(kernel, out_shape=[jax.ShapeDtypeStruct(s, d) for s, d in...]
    dot_general x38 -> x0, matrix products: 252 us -> none  [the longest x2 45 us: forward_image(): jnp.dot(normed_two, expand_w, preferred_element_type=jnp.float32)]
    add x4 -> x0, local copies, waits for them, and re-layouts: 76.4 us -> none  [the longest x2 51.1 us: backward_one_image(): left_part + right_part]
    transpose x19 -> x0, local copies, waits for them, and re-layouts: 69.5 us -> none  [the longest x1 16.4 us: relative_bias(): jnp.einsum('abr,cdrh->hacbd', onehot, partial_sum, precision=PRECISE)]
    unnamed x10 -> x0, waiting for transfers between devices: 56.4 us -> none
    reshape x19 -> x0, local copies, waits for them, and re-layouts: 55.9 us -> none  [the longest x4 23 us: partition(): return shaped.reshape(across * across, WIN * WIN, channels)]
    unnamed x1 -> x0, blocking collectives: 42.1 us -> none
  transfers between devices with their start and end apart: 9 -> 0, of which waited for: 5 -> 0; matrix products, arithmetic and copies ran while one was open for 24% -> 0% of each run, Pallas kernels for 0% -> 0%
where the time goes in v1:
time: 393 us; the launch traced here: 388 us
  Pallas kernels  370 us (94%)
  local copies, waits for them, and re-layouts  14.2 us (4%)
    pallas_call x4, Pallas kernels, call(): pl.pallas_call(kernel, out_shape=[jax.ShapeDtypeStruct(s, d) for s, d in...  184 us
    pallas_call x1, Pallas kernels, scatter_grads(): pl.pallas_call(functools.partial(scatter_kernel, dims), out_shape=[jax.Sh...  97.7 us
    pallas_call x1, Pallas kernels, gather_weights(): pl.pallas_call(functools.partial(gather_kernel, dims), out_shape=[jax.Sha...  88.3 us
    unnamed x9, local copies, waits for them, and re-layouts  7.97 us

profile of v1, /device:TPU:0, one launch (start us, length us, event | category | flops | bytes accessed | tf_op | source)
XLA Modules:
  0.0 388.3 jit_solution(3646638055403332240)
XLA Ops:
  0.6 0.8 stack.35
  1.4 0.8 scatter.12.small
  2.2 0.0 copy-start
  2.2 1.7 copy.41.table
  3.9 1.7 pad_maximum_fusion.mt
  5.6 0.0 copy-done
  5.6 88.3 %gather.1 = (bf16[4,2,2,48,3072]{4,3,2,1,0:T(8,128)(2,1)}, bf16[4,2,2,48,3072]{4,3,2,1,0:T(8,128)(2,1)}, bf16[4,2,2,192,768]{4,3,2,1,0:T(8,128)(2,1)}, f32[8,768]{1,0:T(8,128)}, f32[8,3072]{1,0:T(8,128)}) custom-call(f32[24,3072]{1,0:T(8,128)} %pad_maximum_fusion.mt, f32[24,3072]{1,0:T(8,128)} %me.1, f32[96,768]{1,0:T(8,128)} %mr.1, f32[16,128]{1,0:T(8,128)} %copy-done), custom_call_target="tpu_custom_call" | custom-call | tf_op jit(solution)/shard_map/gather/pallas_call | solution.py:634
  93.9 50.7 %fwd.1 = (bf16[1152,768]{1,0:T(8,128)(2,1)}, bf16[1152,768]{1,0:T(8,128)(2,1)}, bf16[1152,2304]{1,0:T(8,128)(2,1)}, bf16[24,144,1152]{2,1,0:T(8,128)(2,1)}, bf16...) custom-call(s32[2]{0:T(128)} %bitcast.52, bf16[2,576,768]{2,1,0:T(8,128)(2,1)} %bitcast.50, ...), custom_call_target="tpu_custom_call" | custom-call | tf_op jit(solution)/shard_map/fwd/pallas_call | solution.py:199
  144.6 66.5 %ffn.1 = (bf16[2,576,768]{2,1,0:T(8,128)(2,1)}, bf16[1152,768]{1,0:T(8,128)(2,1)}, bf16[3072,768]{1,0:T(8,128)(2,1)}, bf16[768,3072]{1,0:T(8,128)(2,1)}, f32[115...) custom-call(bf16[2,576,768]{2,1,0:T(8,128)(2,1)} %bitcast.49, bf16[576,576]{1,0:T(8,128)(2,1)} %constant.68.clone.perm, ...), custom_call_target="tpu_custom_call" | custom-call | tf_op jit(solution)/shard_map/ffn/pallas_call | solution.py:199
  211.1 0.0 copy-start.1
  211.1 63.8 %bwd.1 = (bf16[2,576,768]{2,1,0:T(8,128)(2,1)}, bf16[768,3072]{1,0:T(8,128)(2,1)}, f32[8,768]{1,0:T(8,128)}, f32[24,576]{1,0:T(8,128)}) custom-call(s32[2]{0:T(128)} %bitcast.53, bf16[576,576]{1,0:T(8,128)(2,1)} %constant.73.clone.unperm, s32[4,144,128]{2,1,0:T(8,128)} %constant.69.clone.raster, s32[8,576]{1,0:T(8,128)} %constant.72.clone.target, ...), custom_call_target="tpu_custom_call" | custom-call | tf_op jit(solution)/shard_map/bwd/pallas_call | solution.py:199
  275.0 0.0 copy-done.1
  275.0 1.4 pad_maximum_fusion.1.sg
  276.3 97.7 %scatter.13 = (f32[24,3072]{1,0:T(8,128)}, f32[24,3072]{1,0:T(8,128)}, f32[96,768]{1,0:T(8,128)}, f32[8,24]{1,0:T(8,128)}, f32[1,96]{1,0:T(1,128)}, /*index=5*/f32[24,576]{1,0:T(8,128)}) custom-call(bf16[4,2,2,48,3072]{4,3,2,1,0:T(8,128)(2,1)} %bitcast.46, bf16[4,2,2,48,3072]{4,3,2,1,0:T(8,128)(2,1)} %bitcast.45, bf16[4,2,2,192,768]{4,3,2,1,0:T(8,128)(2,1)} %bitcast.44, ...), custom_call_target="tpu_custom_call" | custom-call | tf_op jit(solution)/shard_map/scatter/pallas_call | solution.py:839
  374.1 1.5 slice_bitcast_fusion
  375.6 1.5 slice.74
  377.1 1.6 slice.73
  378.7 3.1 table.2
  381.8 1.7 copy.44
  383.5 1.7 copy.49
  385.2 1.7 copy.50
  386.9 1.2 copy.51
  (1 shorter events, 0.0 us)
Async XLA Ops:
  2.2 3.4 copy-start
  211.1 63.9 %copy-start.1 = (f32[1,768]{1,0:T(1,128)S(1)}, f32[1,768]{1,0:T(1,128)}, u32[]{:S(2)}) copy-start(f32[1,768]{1,0:T(1,128)} %get-tuple-element.89) | copy-start | bytes 9220
